TPU v7x, 128 devices: a whole 4x4x4 slice. The times are simulated.
128 devices in a mesh: dp: 16 (over z, y), mp: 8 (over x, core).
Axes of the slice: x: 4, y: 4, z: 4, core: 2. Of those that a mesh axis runs over, the one named last changes fastest.
Arguments:
- residual: bfloat16 [2048, 4096], P('dp', 'mp'), may hold values from -18 to 18
- queries: bfloat16 [2048, 4096], P('dp', 'mp'), may hold values from -20 to 20
- new_keys: bfloat16 [2048, 1024], P('dp', 'mp'), may hold values from -6 to 6
- new_values: bfloat16 [2048, 1024], P('dp', 'mp'), may hold values from -6 to 6
- cache_keys: bfloat16 [2048, 16, 1024], P('dp', None, 'mp'), may hold values from -6 to 6
- cache_values: bfloat16 [2048, 16, 1024], P('dp', None, 'mp'), may hold values from -6 to 6
- cache_len: int32 [1024], replicated, may hold values from 1 to 128, 16384 in all
- page_order: int32 [2048], replicated, may hold values from 0 to 2047, each once
- out_proj: bfloat16 [4096, 4096], P('mp'), may hold values from -0.09375 to 0.09375
- attn_gain: float32 [4096], replicated, may hold values from 0.25 to 1.75
- routes: int32 [2048, 2], P('dp'), may hold values from 0 to 7, all different within a row; in each aligned block of 128 rows (0 to 127, 128 to 255, ...) at most 48 rows name the same one
- route_weight: float32 [2048, 2], P('dp'), may hold values from 0.1 to 1
- gate_proj: bfloat16 [4096, 98304], P(None, ('dp', 'mp')), may hold values from -0.09375 to 0.09375
- up_proj: bfloat16 [4096, 98304], P(None, ('dp', 'mp')), may hold values from -0.09375 to 0.09375
- down_proj: bfloat16 [98304, 4096], P(('dp', 'mp')), may hold values from -0.0546875 to 0.0546875
- final_gain: float32 [4096], P('mp'), may hold values from 0.25 to 1.75
Outputs:
- layer_out: bfloat16 [2048, 4096], P('dp', 'mp')
Inputs may be any that keep to these rules, and one draw needn't show every extreme that they name: `routes`: in each aligned block of 128 rows (the rows of one dp group) no expert is named by more than 48 rows, a bound that some block reaches; a row's two experts differ. `cache_len`: the lengths sum to 16384, and the longest is exactly 128. `page_order`: each page number appears once; pages past the last request's are unused.
All inputs are finite; a program needn't handle non-finite values.
Results may differ from a plain program's by a relative error of at most 0.008.
Values may be sent and summed in bfloat16 or wider, within the bound.
A program may use at most 128 MiB of HBM per device.

v0:
```python
import jax
import jax.numpy as jnp
from jax import lax
from jax.sharding import PartitionSpec as P

D = 4096
HQ = 32
KVH = 8
HD = 128
E = 8
PAGE = 16
DEC = 64
PRE = 64
C = 48
neg_big = -1e30
eps_norm = 1e-05


def page_owner(page_ids, page_order, cache_len):
    page_count = (cache_len + PAGE - 1) // PAGE
    page_ends = jnp.cumsum(page_count)
    page_first = page_ends - page_count
    pool_iota = lax.broadcasted_iota(jnp.int32, (1, page_order.shape[0]), 1)
    order_pos = jnp.sum(jnp.where(page_order[None, :] == page_ids[:, None], pool_iota, 0), axis=1)
    owners = jnp.sum((page_ends[None, :] <= order_pos[:, None]).astype(jnp.int32), axis=1)
    request_iota = lax.broadcasted_iota(jnp.int32, (1, cache_len.shape[0]), 1)
    chosen = request_iota == owners[:, None]
    first_own = jnp.sum(jnp.where(chosen, page_first[None, :], 0), axis=1)
    length_own = jnp.sum(jnp.where(chosen, cache_len[None, :], 0), axis=1)
    offsets = lax.broadcasted_iota(jnp.int32, (1, PAGE), 1)
    key_pos = (order_pos - first_own)[:, None] * PAGE + offsets
    return (owners, key_pos < length_own[:, None])


def page_partials(page_queries, key_pages, value_pages, key_ok, scale):
    scores = (
        jnp.einsum("pkgh,pokh->pkgo", page_queries, key_pages, preferred_element_type=jnp.float32)
        * scale
    )
    wide_mask = key_ok[:, None, None, :]
    masked = jnp.where(wide_mask, scores, neg_big)
    maxima = jnp.max(masked, axis=3)
    weights = jnp.where(wide_mask, jnp.exp(masked - maxima[..., None]), 0.0)
    totals = jnp.sum(weights, axis=3)
    weighted = jnp.einsum(
        "pkgo,pokh->pkgh",
        weights,
        value_pages.astype(jnp.float32),
        precision=lax.Precision.HIGHEST,
        preferred_element_type=jnp.float32,
    )
    return (maxima, totals, weighted)


def fold_pages(maxima, totals, weighted, owned, local_owner):
    top_score = jnp.max(jnp.where(owned[:, :, None, None], maxima[:, None], neg_big), axis=0)
    page_top = top_score[local_owner]
    factors = jnp.exp(maxima - page_top)
    owned_float = owned.astype(jnp.float32)
    sums = jnp.einsum("pr,pkg->rkg", owned_float, totals * factors, precision=lax.Precision.HIGHEST)
    values = jnp.einsum(
        "pr,pkgh->rkgh", owned_float, weighted * factors[..., None], precision=lax.Precision.HIGHEST
    )
    return (top_score, sums, values)


def local(
    residual,
    queries,
    new_keys,
    new_values,
    cache_keys,
    cache_values,
    cache_len,
    page_order,
    out_proj,
    attn_gain,
    routes,
    route_weight,
    gate_proj,
    up_proj,
    down_proj,
    final_gain,
):
    dp_count = lax.axis_size("dp")
    dp_index = lax.axis_index("dp")
    mp_index = lax.axis_index("mp")
    scale = HD ** (-0.5)
    kv_local = new_keys.shape[1] // HD
    group_size = HQ // KVH
    width_local = residual.shape[1]
    pool_local = cache_keys.shape[0]
    request_total = cache_len.shape[0]
    query_heads = queries[:DEC].reshape(DEC, kv_local, group_size, HD)
    gathered = lax.all_gather(queries[:DEC], "dp", axis=0, tiled=True)
    gathered_heads = gathered.reshape(request_total, kv_local, group_size, HD)
    page_ids = dp_index * pool_local + lax.broadcasted_iota(jnp.int32, (pool_local,), 0)
    owners, key_ok = page_owner(page_ids, page_order, cache_len)
    live = owners < request_total
    local_owner = jnp.minimum(owners, request_total - 1)
    key_ok = key_ok & live[:, None]
    key_pages = cache_keys.reshape(pool_local, PAGE, kv_local, HD)
    value_pages = cache_values.reshape(pool_local, PAGE, kv_local, HD)
    page_queries = gathered_heads[local_owner]
    maxima, totals, weighted = page_partials(page_queries, key_pages, value_pages, key_ok, scale)
    owned = (local_owner[:, None] == lax.broadcasted_iota(jnp.int32, (1, request_total), 1)) & live[
        :, None
    ]
    maxima, totals, weighted = fold_pages(maxima, totals, weighted, owned, local_owner)
    maxima = maxima.reshape(dp_count, DEC, kv_local, group_size)
    totals = totals.reshape(dp_count, DEC, kv_local, group_size)
    weighted = weighted.reshape(dp_count, DEC, kv_local, group_size, HD)
    maxima, totals, weighted = (
        lax.all_to_all(maxima, "dp", split_axis=0, concat_axis=0, tiled=True),
        lax.all_to_all(totals, "dp", split_axis=0, concat_axis=0, tiled=True),
        lax.all_to_all(weighted, "dp", split_axis=0, concat_axis=0, tiled=True),
    )
    top_cache = jnp.max(maxima, axis=0)
    factors = jnp.exp(maxima - top_cache[None])
    cache_state = (
        top_cache,
        jnp.sum(totals * factors, axis=0),
        jnp.sum(weighted * factors[..., None], axis=0),
    )
    self_keys = new_keys[:DEC].reshape(DEC, kv_local, HD)
    self_values = new_values[:DEC].reshape(DEC, kv_local, HD).astype(jnp.float32)
    self_score = (
        jnp.einsum("rkgh,rkh->rkg", query_heads, self_keys, preferred_element_type=jnp.float32)
        * scale
    )
    cache_top, cache_total, cache_sum = cache_state
    top_score = jnp.maximum(cache_top, self_score)
    cache_factor = jnp.exp(cache_top - top_score)
    self_factor = jnp.exp(self_score - top_score)
    numerator = (
        cache_sum * cache_factor[..., None] + self_factor[..., None] * self_values[:, :, None, :]
    )
    denominator = cache_total * cache_factor + self_factor
    decode_out = (numerator / denominator[..., None]).astype(jnp.bfloat16).reshape(DEC, -1)
    prompt_q = queries[DEC:].reshape(PRE, kv_local, group_size, HD)
    prompt_k = new_keys[DEC:].reshape(PRE, kv_local, HD)
    prompt_v = new_values[DEC:].reshape(PRE, kv_local, HD).astype(jnp.float32)
    prompt_scores = (
        jnp.einsum("qkgh,tkh->kgqt", prompt_q, prompt_k, preferred_element_type=jnp.float32) * scale
    )
    causal = lax.broadcasted_iota(jnp.int32, (PRE, PRE), 0) >= lax.broadcasted_iota(
        jnp.int32, (PRE, PRE), 1
    )
    masked = jnp.where(causal, prompt_scores, neg_big)
    top_prompt = jnp.max(masked, axis=-1, keepdims=True)
    prompt_weights = jnp.where(causal, jnp.exp(masked - top_prompt), 0.0)
    prompt_num = jnp.einsum(
        "kgqt,tkh->qkgh",
        prompt_weights,
        prompt_v,
        precision=lax.Precision.HIGHEST,
        preferred_element_type=jnp.float32,
    )
    prompt_den = jnp.sum(prompt_weights, axis=-1).transpose(2, 0, 1)
    prompt_out = (prompt_num / prompt_den[..., None]).astype(jnp.bfloat16).reshape(PRE, -1)
    attn = jnp.concatenate([decode_out, prompt_out], axis=0)
    head_terms = jnp.dot(attn, out_proj, preferred_element_type=jnp.float32)
    column_start = mp_index * width_local
    own_columns = lax.dynamic_slice_in_dim(
        head_terms, column_start, width_local, 1
    ) + residual.astype(jnp.float32)
    head_terms = lax.dynamic_update_slice_in_dim(head_terms, own_columns, column_start, 1)
    hidden_full = lax.psum(head_terms, "mp")
    normed = (
        hidden_full
        * lax.rsqrt(jnp.mean(hidden_full * hidden_full, axis=1, keepdims=True) + eps_norm)
        * attn_gain[None, :]
    ).astype(jnp.bfloat16)
    hidden_cols = lax.dynamic_slice_in_dim(hidden_full, column_start, width_local, 1)
    tok_rows = residual.shape[0]
    pairs = routes.reshape(-1)
    onehot = (pairs[:, None] == lax.broadcasted_iota(jnp.int32, (1, E), 1)).astype(jnp.int32)
    slots = jnp.sum((jnp.cumsum(onehot, axis=0) - onehot) * onehot, axis=1)
    target = pairs * C + slots
    cells = lax.broadcasted_iota(jnp.int32, (1, E * C), 1)
    hits = (target[:, None] == cells).reshape(tok_rows, 2, E * C)
    dispatch = jnp.any(hits, axis=1).astype(jnp.bfloat16)
    combine = jnp.sum(jnp.where(hits, route_weight[:, :, None], 0.0), axis=1)
    buffer = lax.dot_general(
        dispatch, normed, (((0,), (0,)), ((), ())), preferred_element_type=jnp.float32
    ).astype(jnp.bfloat16)
    send = jnp.repeat(buffer.reshape(E, C, normed.shape[1]), dp_count // E, axis=0)
    arrived = lax.all_to_all(send, "dp", split_axis=0, concat_axis=0, tiled=True)
    gate_sum = jnp.einsum("scd,df->scf", arrived, gate_proj, preferred_element_type=jnp.float32)
    up_sum = jnp.einsum("scd,df->scf", arrived, up_proj, preferred_element_type=jnp.float32)
    hidden = (jax.nn.silu(gate_sum) * up_sum).astype(jnp.bfloat16)
    down_part = jnp.einsum("scf,fd->scd", hidden, down_proj, preferred_element_type=jnp.float32)
    shares = lax.psum_scatter(
        down_part.astype(jnp.bfloat16), "mp", scatter_dimension=2, tiled=True
    ).astype(jnp.float32)
    returned = lax.all_to_all(shares, "dp", split_axis=0, concat_axis=0, tiled=True)
    back = (
        returned.reshape(E, dp_count // E, C, width_local).sum(axis=1).reshape(E * C, width_local)
    )
    moe_rows = jnp.dot(
        combine, back, precision=lax.Precision.HIGHEST, preferred_element_type=jnp.float32
    )
    mixed = hidden_cols + moe_rows
    square_last = lax.psum(jnp.sum(mixed * mixed, axis=1), "mp")
    scaled = mixed * lax.rsqrt(square_last / D + eps_norm)[:, None] * final_gain[None, :]
    return scaled.astype(jnp.bfloat16)


def solution(mesh):
    return jax.shard_map(
        local,
        mesh=mesh,
        in_specs=(
            P("dp", "mp"),
            P("dp", "mp"),
            P("dp", "mp"),
            P("dp", "mp"),
            P("dp", None, "mp"),
            P("dp", None, "mp"),
            P(),
            P(),
            P("mp", None),
            P(),
            P("dp", None),
            P("dp", None),
            P(None, ("dp", "mp")),
            P(None, ("dp", "mp")),
            P(("dp", "mp"), None),
            P("mp"),
        ),
        out_specs=P("dp", "mp"),
        check_vma=False,
    )
```

profile of v0, /device:TPU:0, one launch (start us, length us, event | category | flops | bytes accessed | tf_op | source)
XLA Modules:
  0.0 386.7 jit_solution(8558500685093032469)
XLA Ops:
  6.5 1.6 fusion.67
  8.2 0.7 fusion.64
  8.9 0.3 reduce-window.15
  9.4 0.8 fusion.63
  10.1 1.0 select_reduce_fusion.1
  11.3 0.9 select_reduce_fusion.3
  12.6 42.3 %all-gather.2.cloned.1.call-done = bf16[1024,512]{1,0:T(8,128)(2,1)} async-done(((bf16[64,512]{1,0:T(8,128)(2,1)}), bf16[1024,512]{1,0:T(8,128)(2,1)}) %all-gather.2.cloned.1.call-update) | async-done | bytes 1048592 | tf_op jit(solution)/shard_map/all_gather | solution.py:95
  54.9 1.3 reshape.430
  56.2 0.7 gather_fusion
  57.0 0.5 fusion.69
  57.5 0.3 select_reduce_fusion
  58.1 0.7 gather_fusion.1
  58.7 0.4 fusion.25
  59.1 0.8 fusion.70
  59.9 0.7 reshape.468
  60.6 4.9 %all-to-all-start.2 = ((f32[16,1,256]{2,1,0:T(1,128)}), f32[16,1,256]{2,1,0:T(1,128)S(1)}, u32[]{:S(2)}, u32[]{:S(2)}) async-start(f32[16,1,256]{2,1,0:T(1,128)} %reshape.468), calls=%async_computation.2 | async-start | bytes 32768 | tf_op jit(solution)/shard_map/all_to_all | solution.py:115
  65.6 0.7 fusion.7
  66.5 0.7 reshape.466
  67.2 5.9 %all-to-all-done.2 = f32[16,1,256]{2,1,0:T(1,128)S(1)} async-done(((f32[16,1,256]{2,1,0:T(1,128)}), f32[16,1,256]{2,1,0:T(1,128)S(1)}, u32[]{:S(2)}, u32[]{:S(2)}) %all-to-all-start.2) | async-done | bytes 16416 | tf_op jit(solution)/shard_map/all_to_all | solution.py:115
  73.1 3.5 all-to-all-start.1
  76.6 2.4 convolution_bitcast_fusion
  79.0 5.1 %all-to-all-done.1 = f32[16,1,256]{2,1,0:T(1,128)S(1)} async-done(((f32[16,1,256]{2,1,0:T(1,128)}), f32[16,1,256]{2,1,0:T(1,128)S(1)}, u32[]{:S(2)}, u32[]{:S(2)}) %all-to-all-start.1) | async-done | bytes 16416 | tf_op jit(solution)/shard_map/all_to_all | solution.py:114
  84.2 3.7 all-to-all-start
  88.6 0.3 fusion.12
  89.0 0.5 broadcast.295
  89.5 0.7 reduce.15
  90.3 0.7 reduce.14
  91.1 24.1 %all-to-all-done = f32[16,64,1,4,128]{4,1,3,2,0:T(8,128)S(1)} async-done(((f32[16,64,1,4,128]{4,1,3,2,0:T(8,128)}), f32[16,64,1,4,128]{4,1,3,2,0:T(8,128)S(1)}, u32[]{:S(2)}, u32[]{:S(2)}) %all-to-all-start) | async-done | bytes 2097184 | tf_op jit(solution)/shard_map/all_to_all | solution.py:116
  115.2 0.7 bitcast_reduce_fusion
  116.1 2.9 fusion.26
  119.1 1.3 copy-done.2
  120.9 0.6 reduce-window.19
  122.2 60.5 %all-reduce.2.cloned.1.call-done = f32[128,4096]{1,0:T(8,128)} async-done(((f32[128,4096]{1,0:T(8,128)}), f32[128,4096]{1,0:T(8,128)}) %all-reduce.2.cloned.1.call-update) | async-done | bytes 2097168 | tf_op jit(solution)/shard_map/psum | solution.py:168
  182.7 2.0 multiply_reduce_fusion
  185.0 1.1 convolution_convert_fusion.1
  186.0 0.8 broadcast_in_dim.146
  186.8 79.0 %all_to_all.25 = bf16[16,48,4096]{2,1,0:T(8,128)(2,1)S(1)} all-to-all(bf16[16,48,4096]{2,1,0:T(8,128)(2,1)S(1)} %bitcast.149), channel_id=1, replica_groups=mesh['dp'=16,'mp'=8] {'dp'}, dimensions={0} | all-to-all | bytes 12582912 | tf_op jit(solution)/shard_map/all_to_all | solution.py:188
  265.8 7.5 %fusion.1 = f32[16,48,768]{2,1,0:T(8,128)S(1)} fusion(bf16[16,48,4096]{2,1,0:T(8,128)(2,1)S(1)} %all_to_all.25, bf16[4096,768]{1,0:T(8,128)(2,1)} %param.29), kind=kOutput, calls=%fused_computation.4 | convolution fusion | flops 4831838208 | bytes 14942208 | tf_op jit(solution)/shard_map/scd,df->scf/dot_general | solution.py:190
  273.3 5.3 %multiply_convert_fusion = bf16[16,48,768]{2,1,0:T(8,128)(2,1)S(1)} fusion(f32[16,48,768]{2,1,0:T(8,128)S(1)} %fusion.1, bf16[16,48,4096]{2,1,0:T(8,128)(2,1)S(1)} %all_to_all.25, bf16[4096,768]{1,0:T(8,128)(2,1)S(1)} %bitcast.157), kind=kOutput, calls=%fused_computation.9 | convolution fusion | flops 4835377152 | bytes 16121856 | tf_op jit(solution)/shard_map/scd,df->scf/dot_general | solution.py:189
  278.7 6.9 %convolution_convert_fusion = bf16[16,48,4096]{2,1,0:T(8,128)(2,1)} fusion(bf16[16,48,768]{2,1,0:T(8,128)(2,1)S(1)} %multiply_convert_fusion, bf16[768,4096]{1,0:T(8,128)(2,1)S(1)} %bitcast.159), kind=kOutput, calls=%fused_computation.2 | convolution fusion | flops 4834983936 | bytes 13762560 | tf_op jit(solution)/shard_map/scf,fd->scd/dot_general | solution.py:192
  285.6 41.4 %reduce-scatter.2.cloned.1.call-done = bf16[16,48,512]{2,1,0:T(8,128)(2,1)} async-done(((bf16[16,48,4096]{2,1,0:T(8,128)(2,1)}), bf16[16,48,512]{2,1,0:T(8,128)(2,1)}) %reduce-scatter.2.cloned.1.call-update) | async-done | bytes 786448 | tf_op jit(solution)/shard_map/reduce_scatter | solution.py:193
  327.0 2.5 convert_element_type.63
  329.5 7.0 %all-to-all-start.4 = ((f32[16,48,512]{2,1,0:T(8,128)}), f32[16,48,512]{2,1,0:T(8,128)}, u32[]{:S(2)}, u32[]{:S(2)}) async-start(f32[16,48,512]{2,1,0:T(8,128)} %convert_element_type.63), calls=%async_computation.5 | async-start | bytes 3145728 | tf_op jit(solution)/shard_map/all_to_all | solution.py:196
  336.7 23.3 %all-to-all-done.4 = f32[16,48,512]{2,1,0:T(8,128)} async-done(((f32[16,48,512]{2,1,0:T(8,128)}), f32[16,48,512]{2,1,0:T(8,128)}, u32[]{:S(2)}, u32[]{:S(2)}) %all-to-all-start.4) | async-done | bytes 1572896 | tf_op jit(solution)/shard_map/all_to_all | solution.py:196
  360.1 1.6 bitcast_reduce_fusion.1
  361.7 0.7 multiply_reduce_fusion.1
  362.4 17.0 %psum.15 = f32[128]{0:T(128)S(1)} all-reduce(f32[128]{0:T(128)S(1)} %get-tuple-element.20), channel_id=1, replica_groups=mesh['dp'=16,'mp'=8] {'mp'}, use_global_device_ids=true, to_apply=%region_24.25 | all-reduce | flops 128 | bytes 1024 | tf_op jit(solution)/shard_map/psum | solution.py:204
  379.4 0.8 multiply_convert_fusion.3
  (93 shorter events, 4.1 us)
Async XLA Ops:
  6.5 59.0 %copy-start = (bf16[128,16,128]{2,1,0:T(8,128)(2,1)S(1)}, bf16[128,16,128]{2,1,0:T(8,128)(2,1)}, u32[]{:S(2)}) copy-start(bf16[128,16,128]{2,1,0:T(8,128)(2,1)} %param.21) | copy-start | bytes 1572868
  6.5 50.5 %copy-start.5 = (bf16[128,16,128]{2,1,0:T(8,128)(2,1)S(1)}, bf16[128,16,128]{2,1,0:T(8,128)(2,1)}, u32[]{:S(2)}) copy-start(bf16[128,16,128]{2,1,0:T(8,128)(2,1)} %param.20) | copy-start | bytes 1572868
  6.5 48.4 %all-gather.2.cloned.1.call-start = ((), (), s32[]{:S(2)}) async-start(), calls=%async_computation.6 | async-start | bytes 1114112 | tf_op jit(solution)/shard_map/all_gather | solution.py:95
  60.6 12.5 %all-to-all-start.2 = ((f32[16,1,256]{2,1,0:T(1,128)}), f32[16,1,256]{2,1,0:T(1,128)S(1)}, u32[]{:S(2)}, u32[]{:S(2)}) async-start(f32[16,1,256]{2,1,0:T(1,128)} %reshape.468), calls=%async_computation.2 | async-start | bytes 32768 | tf_op jit(solution)/shard_map/all_to_all | solution.py:115
  73.1 11.0 %all-to-all-start.1 = ((f32[16,1,256]{2,1,0:T(1,128)}), f32[16,1,256]{2,1,0:T(1,128)S(1)}, u32[]{:S(2)}, u32[]{:S(2)}) async-start(f32[16,1,256]{2,1,0:T(1,128)} %reshape.466), calls=%async_computation.1 | async-start | bytes 32768 | tf_op jit(solution)/shard_map/all_to_all | solution.py:114
  79.0 8.9 %copy-start.4 = (bf16[64,512]{1,0:T(8,128)(2,1)S(1)}, bf16[64,512]{1,0:T(8,128)(2,1)}, u32[]{:S(2)}) copy-start(bf16[64,512]{1,0:T(8,128)(2,1)} %get-tuple-element.12) | copy-start | bytes 196612
  79.0 9.0 %copy-start.7 = (bf16[128,128]{1,0:T(8,128)(2,1)S(1)}, bf16[128,128]{1,0:T(8,128)(2,1)}, u32[]{:S(2)}) copy-start(bf16[128,128]{1,0:T(8,128)(2,1)} %param.18) | copy-start | bytes 98308
  79.0 9.5 %copy-start.9 = (bf16[128,128]{1,0:T(8,128)(2,1)S(1)}, bf16[128,128]{1,0:T(8,128)(2,1)}, u32[]{:S(2)}) copy-start(bf16[128,128]{1,0:T(8,128)(2,1)} %param.19) | copy-start | bytes 98308
  84.2 31.0 %all-to-all-start = ((f32[16,64,1,4,128]{4,1,3,2,0:T(8,128)}), f32[16,64,1,4,128]{4,1,3,2,0:T(8,128)S(1)}, u32[]{:S(2)}, u32[]{:S(2)}) async-start(f32[16,64,1,4,128]{4,1,3,2,0:T(8,128)} %convolution_bitcast_fusion), calls=%async_computation | async-start | bytes 4194304 | tf_op jit(solution)/shard_map/all_to_all | solution.py:116
  87.9 94.8 %all-reduce.2.cloned.1.call-start = ((), (), s32[]{:S(2)}) async-start(), calls=%async_computation.7 | async-start | bytes 4194304 | tf_op jit(solution)/shard_map/psum | solution.py:168
  116.1 3.0 copy-start.6
  119.0 1.4 copy-start.10
  119.1 1.3 copy-start.2
  119.1 65.6 %copy-start.8 = (f32[4096]{0:T(1024)S(1)}, f32[4096]{0:T(1024)}, u32[]{:S(2)}) copy-start(f32[4096]{0:T(1024)} %param.25) | copy-start | bytes 49156
  120.4 206.6 %reduce-scatter.2.cloned.1.call-start = ((), (), s32[]{:S(2)}) async-start(), calls=%async_computation.8 | async-start | bytes 7077888 | tf_op jit(solution)/shard_map/reduce_scatter | solution.py:193
  182.7 2.2 copy-start.3
  186.8 86.5 %slice-start = ((s8[6291456]{0:T(1024)(128)(4,1)}), s8[4194304]{0:T(1024)(128)(4,1)S(1)}, s32[]{:S(2)}) async-start(s8[6291456]{0:T(1024)(128)(4,1)} %bitcast.156), calls=%async_computation.9 | async-start | bytes 8388608
  265.8 7.5 %slice-start.1 = ((s8[6291456]{0:T(1024)(128)(4,1)}), s8[2097152]{0:T(1024)(128)(4,1)S(1)}, s32[]{:S(2)}) async-start(s8[6291456]{0:T(1024)(128)(4,1)} %bitcast.156), calls=%async_computation.10 | async-start | bytes 4194304
  265.8 12.8 %slice-start.2 = ((s8[6291456]{0:T(1024)(128)(4,1)}), s8[4194304]{0:T(1024)(128)(4,1)S(1)}, s32[]{:S(2)}) async-start(s8[6291456]{0:T(1024)(128)(4,1)} %bitcast.158), calls=%async_computation.11 | async-start | bytes 8388608
  273.3 5.3 %slice-start.3 = ((s8[6291456]{0:T(1024)(128)(4,1)}), s8[2097152]{0:T(1024)(128)(4,1)S(1)}, s32[]{:S(2)}) async-start(s8[6291456]{0:T(1024)(128)(4,1)} %bitcast.158), calls=%async_computation.12 | async-start | bytes 4194304
  285.6 51.0 %copy-start.12 = (f32[128,2]{0,1:T(2,128)S(1)}, f32[128,2]{0,1:T(2,128)}, u32[]{:S(2)}) copy-start(f32[128,2]{0,1:T(2,128)} %param.27) | copy-start | bytes 3076
  329.5 30.5 %all-to-all-start.4 = ((f32[16,48,512]{2,1,0:T(8,128)}), f32[16,48,512]{2,1,0:T(8,128)}, u32[]{:S(2)}, u32[]{:S(2)}) async-start(f32[16,48,512]{2,1,0:T(8,128)} %convert_element_type.63), calls=%async_computation.5 | async-start | bytes 3145728 | tf_op jit(solution)/shard_map/all_to_all | solution.py:196
  336.6 42.8 %copy-start.11 = (f32[512]{0:T(512)S(1)}, f32[512]{0:T(512)}, u32[]{:S(2)}) copy-start(f32[512]{0:T(512)} %param.31) | copy-start | bytes 6148
  336.6 43.6 %copy-start.1 = (bf16[128,16,128]{2,1,0:T(8,128)(2,1)S(1)}, bf16[128,16,128]{2,1,0:T(8,128)(2,1)}, u32[]{:S(2)}) copy-start(bf16[128,16,128]{2,1,0:T(8,128)(2,1)} %param.21) | copy-start | bytes 1572868
Sparse Core Ops, SparseCore 0:
  9.5 45.3 all-gather.1
  120.5 62.1 all-reduce.1
  285.7 41.2 reduce-scatter.1
where the time goes:
time: 387 us
  waiting for transfers between devices  203 us (52%)
  blocking collectives  96 us (25%)
  matrix products  29.4 us (8%)
  starting transfers between devices  19.3 us (5%)
  other arithmetic  15.1 us (4%)
  between operations  13.6 us (4%)
  local copies, waits for them, and re-layouts  10.6 us (3%)
    all_to_all x1, blocking collectives, local(): lax.all_to_all(send, 'dp', split_axis=0, concat_axis=0, tiled=True)  79 us
    psum x1, waiting for transfers between devices, local(): hidden_full = lax.psum(head_terms, 'mp')  60.5 us
    all_gather x1, waiting for transfers between devices, local(): gathered = lax.all_gather(queries[:DEC], 'dp', axis=0, tiled=True)  42.3 us
    reduce_scatter x1, waiting for transfers between devices, local(): lax.psum_scatter(down_part.astype(jnp.bfloat16), 'mp', scatter_dimension=...  41.4 us
    all_to_all x1, waiting for transfers between devices, local(): lax.all_to_all(weighted, 'dp', split_axis=0, concat_axis=0, tiled=True)  24.1 us
    all_to_all x1, waiting for transfers between devices, local(): lax.all_to_all(shares, 'dp', split_axis=0, concat_axis=0, tiled=True)  23.3 us
    psum x1, blocking collectives, local(): square_last = lax.psum(jnp.sum(mixed * mixed, axis=1), 'mp')  17 us
  transfers between devices with their start and end apart: 7, of which 7 were waited for; matrix products, arithmetic and copies ran while one was open for 3% of the time, Pallas kernels for 0%

commit v1 on v0

--- a/solution.py
+++ b/solution.py
@@ -165,7 +165,7 @@
         head_terms, column_start, width_local, 1
     ) + residual.astype(jnp.float32)
     head_terms = lax.dynamic_update_slice_in_dim(head_terms, own_columns, column_start, 1)
-    hidden_full = lax.psum(head_terms, "mp")
+    hidden_full = jnp.sum(lax.all_gather(head_terms, axis_name="mp"), axis=0)
     normed = (
         hidden_full
         * lax.rsqrt(jnp.mean(hidden_full * hidden_full, axis=1, keepdims=True) + eps_norm)

time: 387 us -> 413 us (1.067)
  waiting for transfers between devices: 203 us -> 220 us
  other arithmetic: 15.1 us -> 20.7 us
    all_gather x0 -> x1, waiting for transfers between devices: none -> 79.8 us  [local(): hidden_full = jnp.sum(lax.all_gather(head_terms, axis_name='mp'), axis=0)]
    psum x1 -> x0, waiting for transfers between devices: 60.5 us -> none  [local(): hidden_full = lax.psum(head_terms, 'mp')]
    reduce_sum x0 -> x1, other arithmetic: none -> 7.36 us  [local(): hidden_full = jnp.sum(lax.all_gather(head_terms, axis_name='mp'), axis=0)]
where the time goes in v1:
time: 413 us; the launch traced here: 412 us
  waiting for transfers between devices  220 us (53%)
  blocking collectives  97.8 us (24%)
  matrix products  29.4 us (7%)
  other arithmetic  20.7 us (5%)
  starting transfers between devices  19.2 us (5%)
  between operations  13.6 us (3%)
  local copies, waits for them, and re-layouts  11.3 us (3%)
    all_to_all x1, blocking collectives, local(): lax.all_to_all(send, 'dp', split_axis=0, concat_axis=0, tiled=True)  80.8 us
    all_gather x1, waiting for transfers between devices, local(): hidden_full = jnp.sum(lax.all_gather(head_terms, axis_name='mp'), axis=0)  79.8 us
    all_gather x1, waiting for transfers between devices, local(): gathered = lax.all_gather(queries[:DEC], 'dp', axis=0, tiled=True)  42.3 us
    reduce_scatter x1, waiting for transfers between devices, local(): lax.psum_scatter(down_part.astype(jnp.bfloat16), 'mp', scatter_dimension=...  39.3 us
    all_to_all x1, waiting for transfers between devices, local(): lax.all_to_all(weighted, 'dp', split_axis=0, concat_axis=0, tiled=True)  24.1 us
    all_to_all x1, waiting for transfers between devices, local(): lax.all_to_all(shares, 'dp', split_axis=0, concat_axis=0, tiled=True)  23.3 us
    psum x1, blocking collectives, local(): square_last = lax.psum(jnp.sum(mixed * mixed, axis=1), 'mp')  17 us
  transfers between devices with their start and end apart: 7, of which 7 were waited for; matrix products, arithmetic and copies ran while one was open for 3% of the time, Pallas kernels for 0%

profile of v1, /device:TPU:0, one launch (start us, length us, event | category | flops | bytes accessed | tf_op | source)
XLA Modules:
  0.0 411.8 jit_solution(2624498678209332277)
XLA Ops:
  6.5 1.6 fusion.67
  8.2 0.7 fusion.64
  9.4 0.8 fusion.63
  10.1 1.0 select_reduce_fusion.1
  11.3 0.9 select_reduce_fusion.3
  12.6 42.3 %all-gather.3.cloned.1.call-done = bf16[1024,512]{1,0:T(8,128)(2,1)} async-done(((bf16[64,512]{1,0:T(8,128)(2,1)}), bf16[1024,512]{1,0:T(8,128)(2,1)}) %all-gather.3.cloned.1.call-update) | async-done | bytes 1048592 | tf_op jit(solution)/shard_map/all_gather | solution.py:95
  54.9 1.3 reshape.432
  56.2 0.7 gather_fusion
  57.0 0.5 fusion.69
  57.5 0.3 select_reduce_fusion
  58.1 0.7 gather_fusion.1
  58.7 0.4 fusion.25
  59.1 0.8 fusion.70
  59.9 0.7 reshape.470
  60.6 4.9 %all-to-all-start.2 = ((f32[16,1,256]{2,1,0:T(1,128)}), f32[16,1,256]{2,1,0:T(1,128)S(1)}, u32[]{:S(2)}, u32[]{:S(2)}) async-start(f32[16,1,256]{2,1,0:T(1,128)} %reshape.470), calls=%async_computation.2 | async-start | bytes 32768 | tf_op jit(solution)/shard_map/all_to_all | solution.py:115
  65.6 0.7 fusion.7
  66.5 0.7 reshape.468
  67.2 5.9 %all-to-all-done.2 = f32[16,1,256]{2,1,0:T(1,128)S(1)} async-done(((f32[16,1,256]{2,1,0:T(1,128)}), f32[16,1,256]{2,1,0:T(1,128)S(1)}, u32[]{:S(2)}, u32[]{:S(2)}) %all-to-all-start.2) | async-done | bytes 16416 | tf_op jit(solution)/shard_map/all_to_all | solution.py:115
  73.1 3.5 all-to-all-start.1
  76.6 2.4 convolution_bitcast_fusion
  79.0 5.1 %all-to-all-done.1 = f32[16,1,256]{2,1,0:T(1,128)S(1)} async-done(((f32[16,1,256]{2,1,0:T(1,128)}), f32[16,1,256]{2,1,0:T(1,128)S(1)}, u32[]{:S(2)}, u32[]{:S(2)}) %all-to-all-start.1) | async-done | bytes 16416 | tf_op jit(solution)/shard_map/all_to_all | solution.py:114
  84.2 3.7 all-to-all-start
  88.6 0.3 fusion.12
  89.0 0.5 broadcast.295
  89.5 0.7 reduce.15
  90.3 0.7 reduce.14
  91.1 24.1 %all-to-all-done = f32[16,64,1,4,128]{4,1,3,2,0:T(8,128)S(1)} async-done(((f32[16,64,1,4,128]{4,1,3,2,0:T(8,128)}), f32[16,64,1,4,128]{4,1,3,2,0:T(8,128)S(1)}, u32[]{:S(2)}, u32[]{:S(2)}) %all-to-all-start) | async-done | bytes 2097184 | tf_op jit(solution)/shard_map/all_to_all | solution.py:116
  115.2 0.7 bitcast_reduce_fusion
  116.1 2.9 fusion.26
  119.2 0.7 copy-done.5
  119.9 1.3 copy-done.2
  121.8 0.6 reduce-window.19
  123.1 79.8 %all-gather.5.cloned.1.call-done = f32[8,128,4096]{2,1,0:T(8,128)} async-done(((f32[1,128,4096]{2,1,0:T(8,128)}), f32[8,128,4096]{2,1,0:T(8,128)}) %all-gather.5.cloned.1.call-update) | async-done | bytes 16777232 | tf_op jit(solution)/shard_map/all_gather | solution.py:168
  202.9 7.4 %reduce_sum.139 = f32[128,4096]{1,0:T(8,128)S(1)} reduce(f32[8,128,4096]{2,1,0:T(8,128)} %all-gather.5.cloned.1.call-done, f32[]{:T(128)} %constant.69.clone.1), dimensions={0}, to_apply=%region_14.15 | reduce | flops 3670016 | bytes 18874372 | tf_op jit(solution)/shard_map/reduce_sum | solution.py:168
  210.5 1.1 convolution_convert_fusion.1
  211.5 0.8 broadcast_in_dim.146
  212.3 80.8 %all_to_all.25 = bf16[16,48,4096]{2,1,0:T(8,128)(2,1)S(1)} all-to-all(bf16[16,48,4096]{2,1,0:T(8,128)(2,1)S(1)} %bitcast.152), channel_id=1, replica_groups=mesh['dp'=16,'mp'=8] {'dp'}, dimensions={0} | all-to-all | bytes 12582912 | tf_op jit(solution)/shard_map/all_to_all | solution.py:188
  293.1 7.5 %fusion.1 = f32[16,48,768]{2,1,0:T(8,128)S(1)} fusion(bf16[16,48,4096]{2,1,0:T(8,128)(2,1)S(1)} %all_to_all.25, bf16[4096,768]{1,0:T(8,128)(2,1)} %param.29), kind=kOutput, calls=%fused_computation.4 | convolution fusion | flops 4831838208 | bytes 14942208 | tf_op jit(solution)/shard_map/scd,df->scf/dot_general | solution.py:190
  300.6 5.3 %multiply_convert_fusion = bf16[16,48,768]{2,1,0:T(8,128)(2,1)S(1)} fusion(f32[16,48,768]{2,1,0:T(8,128)S(1)} %fusion.1, bf16[16,48,4096]{2,1,0:T(8,128)(2,1)S(1)} %all_to_all.25, bf16[4096,768]{1,0:T(8,128)(2,1)S(1)} %bitcast.161), kind=kOutput, calls=%fused_computation.9 | convolution fusion | flops 4835377152 | bytes 16121856 | tf_op jit(solution)/shard_map/scd,df->scf/dot_general | solution.py:189
  306.0 6.9 %convolution_convert_fusion = bf16[16,48,4096]{2,1,0:T(8,128)(2,1)} fusion(bf16[16,48,768]{2,1,0:T(8,128)(2,1)S(1)} %multiply_convert_fusion, bf16[768,4096]{1,0:T(8,128)(2,1)S(1)} %bitcast.163), kind=kOutput, calls=%fused_computation.2 | convolution fusion | flops 4834983936 | bytes 13762560 | tf_op jit(solution)/shard_map/scf,fd->scd/dot_general | solution.py:192
  312.9 39.3 %reduce-scatter.2.cloned.1.call-done = bf16[16,48,512]{2,1,0:T(8,128)(2,1)} async-done(((bf16[16,48,4096]{2,1,0:T(8,128)(2,1)}), bf16[16,48,512]{2,1,0:T(8,128)(2,1)}) %reduce-scatter.2.cloned.1.call-update) | async-done | bytes 786448 | tf_op jit(solution)/shard_map/reduce_scatter | solution.py:193
  352.2 2.5 convert_element_type.63
  354.7 7.0 %all-to-all-start.4 = ((f32[16,48,512]{2,1,0:T(8,128)}), f32[16,48,512]{2,1,0:T(8,128)}, u32[]{:S(2)}, u32[]{:S(2)}) async-start(f32[16,48,512]{2,1,0:T(8,128)} %convert_element_type.63), calls=%async_computation.5 | async-start | bytes 3145728 | tf_op jit(solution)/shard_map/all_to_all | solution.py:196
  361.9 23.3 %all-to-all-done.4 = f32[16,48,512]{2,1,0:T(8,128)} async-done(((f32[16,48,512]{2,1,0:T(8,128)}), f32[16,48,512]{2,1,0:T(8,128)}, u32[]{:S(2)}, u32[]{:S(2)}) %all-to-all-start.4) | async-done | bytes 1572896 | tf_op jit(solution)/shard_map/all_to_all | solution.py:196
  385.2 1.6 bitcast_reduce_fusion.1
  386.8 0.7 multiply_reduce_fusion.1
  387.6 17.0 %psum.7 = f32[128]{0:T(128)S(1)} all-reduce(f32[128]{0:T(128)S(1)} %get-tuple-element.20), channel_id=1, replica_groups=mesh['dp'=16,'mp'=8] {'mp'}, use_global_device_ids=true, to_apply=%region_24.25 | all-reduce | flops 128 | bytes 1024 | tf_op jit(solution)/shard_map/psum | solution.py:204
  404.5 0.8 multiply_convert_fusion.3
  (93 shorter events, 4.5 us)
Async XLA Ops:
  6.5 59.0 %copy-start = (bf16[128,16,128]{2,1,0:T(8,128)(2,1)S(1)}, bf16[128,16,128]{2,1,0:T(8,128)(2,1)}, u32[]{:S(2)}) copy-start(bf16[128,16,128]{2,1,0:T(8,128)(2,1)} %param.21) | copy-start | bytes 1572868
  6.5 50.5 %copy-start.4 = (bf16[128,16,128]{2,1,0:T(8,128)(2,1)S(1)}, bf16[128,16,128]{2,1,0:T(8,128)(2,1)}, u32[]{:S(2)}) copy-start(bf16[128,16,128]{2,1,0:T(8,128)(2,1)} %param.20) | copy-start | bytes 1572868
  6.5 48.4 %all-gather.3.cloned.1.call-start = ((), (), s32[]{:S(2)}) async-start(), calls=%async_computation.6 | async-start | bytes 1114112 | tf_op jit(solution)/shard_map/all_gather | solution.py:95
  60.6 12.5 %all-to-all-start.2 = ((f32[16,1,256]{2,1,0:T(1,128)}), f32[16,1,256]{2,1,0:T(1,128)S(1)}, u32[]{:S(2)}, u32[]{:S(2)}) async-start(f32[16,1,256]{2,1,0:T(1,128)} %reshape.470), calls=%async_computation.2 | async-start | bytes 32768 | tf_op jit(solution)/shard_map/all_to_all | solution.py:115
  73.1 11.0 %all-to-all-start.1 = ((f32[16,1,256]{2,1,0:T(1,128)}), f32[16,1,256]{2,1,0:T(1,128)S(1)}, u32[]{:S(2)}, u32[]{:S(2)}) async-start(f32[16,1,256]{2,1,0:T(1,128)} %reshape.468), calls=%async_computation.1 | async-start | bytes 32768 | tf_op jit(solution)/shard_map/all_to_all | solution.py:114
  79.0 8.9 %copy-start.3 = (bf16[64,512]{1,0:T(8,128)(2,1)S(1)}, bf16[64,512]{1,0:T(8,128)(2,1)}, u32[]{:S(2)}) copy-start(bf16[64,512]{1,0:T(8,128)(2,1)} %get-tuple-element.12) | copy-start | bytes 196612
  79.0 9.0 %copy-start.6 = (bf16[128,128]{1,0:T(8,128)(2,1)S(1)}, bf16[128,128]{1,0:T(8,128)(2,1)}, u32[]{:S(2)}) copy-start(bf16[128,128]{1,0:T(8,128)(2,1)} %param.18) | copy-start | bytes 98308
  79.0 9.5 %copy-start.8 = (bf16[128,128]{1,0:T(8,128)(2,1)S(1)}, bf16[128,128]{1,0:T(8,128)(2,1)}, u32[]{:S(2)}) copy-start(bf16[128,128]{1,0:T(8,128)(2,1)} %param.19) | copy-start | bytes 98308
  84.2 31.0 %all-to-all-start = ((f32[16,64,1,4,128]{4,1,3,2,0:T(8,128)}), f32[16,64,1,4,128]{4,1,3,2,0:T(8,128)S(1)}, u32[]{:S(2)}, u32[]{:S(2)}) async-start(f32[16,64,1,4,128]{4,1,3,2,0:T(8,128)} %convolution_bitcast_fusion), calls=%async_computation | async-start | bytes 4194304 | tf_op jit(solution)/shard_map/all_to_all | solution.py:116
  87.9 115.0 %all-gather.5.cloned.1.call-start = ((), (), s32[]{:S(2)}) async-start(), calls=%async_computation.7 | async-start | bytes 18874368 | tf_op jit(solution)/shard_map/all_gather | solution.py:168
  119.0 0.9 copy-start.5
  119.9 1.5 copy-start.9
  119.9 1.4 copy-start.2
  121.3 230.9 %reduce-scatter.2.cloned.1.call-start = ((), (), s32[]{:S(2)}) async-start(), calls=%async_computation.8 | async-start | bytes 7077888 | tf_op jit(solution)/shard_map/reduce_scatter | solution.py:193
  123.1 87.4 %copy-start.7 = (f32[4096]{0:T(1024)S(1)}, f32[4096]{0:T(1024)}, u32[]{:S(2)}) copy-start(f32[4096]{0:T(1024)} %param.25) | copy-start | bytes 49156
  212.3 88.3 %slice-start = ((s8[6291456]{0:T(1024)(128)(4,1)}), s8[4194304]{0:T(1024)(128)(4,1)S(1)}, s32[]{:S(2)}) async-start(s8[6291456]{0:T(1024)(128)(4,1)} %bitcast.160), calls=%async_computation.9 | async-start | bytes 8388608
  293.1 7.5 %slice-start.1 = ((s8[6291456]{0:T(1024)(128)(4,1)}), s8[2097152]{0:T(1024)(128)(4,1)S(1)}, s32[]{:S(2)}) async-start(s8[6291456]{0:T(1024)(128)(4,1)} %bitcast.160), calls=%async_computation.10 | async-start | bytes 4194304
  293.1 12.8 %slice-start.2 = ((s8[6291456]{0:T(1024)(128)(4,1)}), s8[4194304]{0:T(1024)(128)(4,1)S(1)}, s32[]{:S(2)}) async-start(s8[6291456]{0:T(1024)(128)(4,1)} %bitcast.162), calls=%async_computation.11 | async-start | bytes 8388608
  300.6 5.3 %slice-start.3 = ((s8[6291456]{0:T(1024)(128)(4,1)}), s8[2097152]{0:T(1024)(128)(4,1)S(1)}, s32[]{:S(2)}) async-start(s8[6291456]{0:T(1024)(128)(4,1)} %bitcast.162), calls=%async_computation.12 | async-start | bytes 4194304
  312.9 48.8 %copy-start.11 = (f32[128,2]{0,1:T(2,128)S(1)}, f32[128,2]{0,1:T(2,128)}, u32[]{:S(2)}) copy-start(f32[128,2]{0,1:T(2,128)} %param.27) | copy-start | bytes 3076
  354.7 30.5 %all-to-all-start.4 = ((f32[16,48,512]{2,1,0:T(8,128)}), f32[16,48,512]{2,1,0:T(8,128)}, u32[]{:S(2)}, u32[]{:S(2)}) async-start(f32[16,48,512]{2,1,0:T(8,128)} %convert_element_type.63), calls=%async_computation.5 | async-start | bytes 3145728 | tf_op jit(solution)/shard_map/all_to_all | solution.py:196
  361.7 42.8 %copy-start.10 = (f32[512]{0:T(512)S(1)}, f32[512]{0:T(512)}, u32[]{:S(2)}) copy-start(f32[512]{0:T(512)} %param.31) | copy-start | bytes 6148
  361.7 43.6 %copy-start.1 = (bf16[128,16,128]{2,1,0:T(8,128)(2,1)S(1)}, bf16[128,16,128]{2,1,0:T(8,128)(2,1)}, u32[]{:S(2)}) copy-start(bf16[128,16,128]{2,1,0:T(8,128)(2,1)} %param.21) | copy-start | bytes 1572868
Sparse Core Ops, SparseCore 0:
  9.5 45.3 all-gather.2
  121.4 81.3 all-gather.4
  313.0 39.1 reduce-scatter.1
